TPU v7x, 32 devices: a whole 2x2x4 slice. The times are simulated.
32 devices in a mesh: space: 4 (over y, x), vel: 8 (over z, core).
Axes of the slice: x: 2, y: 2, z: 4, core: 2. Of those that a mesh axis runs over, the one named last changes fastest.
Arguments:
- cotangent: float32 [8192, 128, 128], P('vel', 'space'), may hold values from -6 to 6
- speed: float32 [3, 8192], P(None, 'vel'), may hold values from 0.1 to 3
- direction: int32 [3, 8192], P(None, 'vel'), may hold values from 0 to 1
- macroscopic_record: float32 [3, 5, 128, 128], P(None, None, 'space'), may hold values from -1 to 2, as said below
Outputs:
- gradient: float32 [8192, 128, 128], P('vel', 'space')
Inputs may be any that keep to these rules, and one draw needn't show every extreme that they name: `direction`: 1 marks a positive velocity component, 0 a negative one. `macroscopic_record`: density and temperature lie between 0.5 and 2, flow velocity components between -1 and 1.
All inputs are finite; a program needn't handle non-finite values.
Results may differ from a plain program's by a relative error of at most 0.00013.
Values sent between devices are 32-bit elements; how exact they have to be, the bound alone decides.
No kernel may reach another device: no remote copies, remote signals or barrier semaphores. Data moves between devices by JAX's collectives and lax.ppermute only.
A program may use at most 128 MiB of HBM per device.

v0:
```python
import math
import jax
import jax.numpy as jnp
from jax import lax
from jax.sharding import PartitionSpec as P

SPEED_POINTS = 8192
STEPS = 3
courant_number = 0.1
region_capacity = 216.0
mode_gains = (
    1.0,
    1.0,
    1.0,
    1.0,
    1.0,
    -0.5,
    -0.5,
    -0.5,
    -0.5,
    -0.5,
    1.0 / 3.0,
    1.0 / 3.0,
    1.0 / 3.0,
)
monomials = [
    (first, second, degree - first - second)
    for degree in range(4)
    for first in range(degree, -1, -1)
    for second in range(degree - first, -1, -1)
]
monomial_place = {exponents: place for place, exponents in enumerate(monomials)}


def with_halo(x, sides, width):
    for axis, dim in sides:
        peers, length = (lax.axis_size(axis), x.shape[dim])
        up = [(i, (i + 1) % peers) for i in range(peers)]
        down = [(j, i) for i, j in up]
        last = lax.slice_in_dim(x, length - width, length, axis=dim)
        first = lax.slice_in_dim(x, 0, width, axis=dim)
        before = lax.ppermute(last, axis, up)
        after = lax.ppermute(first, axis, down)
        x = jnp.concatenate([before, x, after], axis=dim)
    return x


def raise_to(values, exponent):
    result = jnp.ones_like(values)
    for repeat in range(exponent):
        result = result * values
    return result


def poly_mul(left, right):
    result = {}
    for left_key, left_coef in left.items():
        for right_key, right_coef in right.items():
            joined = (
                left_key[0] + right_key[0],
                left_key[1] + right_key[1],
                left_key[2] + right_key[2],
            )
            product = left_coef * right_coef
            result[joined] = result[joined] + product if joined in result else product
    return result


def poly_comb(terms):
    result = {}
    for weight, poly in terms:
        for poly_key, poly_coef in poly.items():
            scaled = weight * poly_coef
            result[poly_key] = result[poly_key] + scaled if poly_key in result else scaled
    return result


def hermite_polys(flow_rows, reciprocal_factor):
    linear = []
    for component in range(3):
        unit_key = tuple((1 if other == component else 0 for other in range(3)))
        linear.append(
            {unit_key: reciprocal_factor, (0, 0, 0): -flow_rows[component] * reciprocal_factor}
        )
    comp_x, comp_y, comp_z = linear
    unit_poly = {(0, 0, 0): 1.0}
    square_x = poly_mul(comp_x, comp_x)
    square_y = poly_mul(comp_y, comp_y)
    square_z = poly_mul(comp_z, comp_z)
    square = poly_comb([(1.0, square_x), (1.0, square_y), (1.0, square_z)])
    shifted = poly_comb([(1.0, square), (-5.0, unit_poly)])
    heat_scale = 1.0 / math.sqrt(10.0)
    return [
        unit_poly,
        comp_x,
        comp_y,
        comp_z,
        poly_comb([(1.0 / math.sqrt(6.0), square), (-3.0 / math.sqrt(6.0), unit_poly)]),
        poly_mul(comp_x, comp_y),
        poly_mul(comp_x, comp_z),
        poly_mul(comp_y, comp_z),
        poly_comb([(0.5, square_x), (-0.5, square_y)]),
        poly_comb(
            [
                (1.0 / math.sqrt(12.0), square_x),
                (1.0 / math.sqrt(12.0), square_y),
                (-2.0 / math.sqrt(12.0), square_z),
            ]
        ),
        poly_comb([(heat_scale, poly_mul(comp_x, shifted))]),
        poly_comb([(heat_scale, poly_mul(comp_y, shifted))]),
        poly_comb([(heat_scale, poly_mul(comp_z, shifted))]),
    ]


def to_modes(raw_rows, polys, zeros_like):
    mode_rows = []
    for poly in polys:
        running = zeros_like
        for poly_key, poly_coef in poly.items():
            running = running + poly_coef * raw_rows[monomial_place[poly_key]]
        mode_rows.append(running)
    return mode_rows


def to_coeffs(mode_rows, polys, zeros_like):
    coeff_rows = [zeros_like for exponents in monomials]
    for mode_index, poly in enumerate(polys):
        scaled_mode = mode_gains[mode_index] * mode_rows[mode_index]
        for poly_key, poly_coef in poly.items():
            place = monomial_place[poly_key]
            coeff_rows[place] = coeff_rows[place] + poly_coef * scaled_mode
    return jnp.stack(coeff_rows)


def pad_both(values, along):
    extent = values.shape[along]
    lower_rim = lax.slice_in_dim(values, extent - 2, extent, axis=along)
    upper_rim = lax.slice_in_dim(values, 0, 2, axis=along)
    return jnp.concatenate([lower_rim, values, upper_rim], axis=along)


def upwind_back(padded, length, along, lam_col, positive):

    def window(start_at):
        return lax.slice_in_dim(padded, start_at, start_at + length, axis=along)

    center = window(2)
    nearer = jnp.where(positive, window(3), window(1))
    farther = jnp.where(positive, window(4), window(0))
    return center - 0.5 * lam_col * (3.0 * center - 4.0 * nearer + farther)


def shards(cotangent, speed, direction, macroscopic_record):
    rows_x = cotangent.shape[1]
    cols_y = cotangent.shape[2]
    velocity = (2 * direction - 1).astype(jnp.float32) * speed
    factors = courant_number * speed
    positive = direction > 0
    lam_x = factors[0][:, None, None]
    lam_y = factors[1][:, None, None]
    pos_x = positive[0][:, None, None]
    pos_y = positive[1][:, None, None]
    table = jnp.stack(
        [
            raise_to(velocity[0], exponents[0])
            * raise_to(velocity[1], exponents[1])
            * raise_to(velocity[2], exponents[2])
            for exponents in monomials
        ]
    )
    adjoint = cotangent
    for iteration_counter in range(STEPS - 1, -1, -1):
        moved_y = upwind_back(pad_both(adjoint, 2), cols_y, 2, lam_y, pos_y)
        padded_x = with_halo(moved_y, (("space", 1),), 2)
        advected = upwind_back(padded_x, rows_x, 1, lam_x, pos_x)
        particle_concentration = macroscopic_record[iteration_counter, 0]
        flow_rows = [macroscopic_record[iteration_counter, 1 + component] for component in range(3)]
        thermal_energy_level = macroscopic_record[iteration_counter, 4]
        reciprocal_factor = 1.0 / jnp.sqrt(thermal_energy_level)
        normalising_coefficient = (
            particle_concentration
            * (2.0 * math.pi * thermal_energy_level) ** (-1.5)
            * region_capacity
            / SPEED_POINTS
        )
        relaxation_rate = 0.3 * particle_concentration * jnp.sqrt(thermal_energy_level)
        peculiar = [
            (velocity[component][:, None, None] - flow_rows[component]) * reciprocal_factor
            for component in range(3)
        ]
        weight = normalising_coefficient * jnp.exp(
            -0.5 * (peculiar[0] ** 2 + peculiar[1] ** 2 + peculiar[2] ** 2)
        )
        raw_moments = jnp.einsum(
            "av,vxy->axy", table, weight * advected, precision=lax.Precision.HIGHEST
        )
        zero_cells = jnp.zeros_like(particle_concentration)
        summed = lax.psum(raw_moments, "vel")
        polys = hermite_polys(flow_rows, reciprocal_factor)
        coeffs = to_coeffs(to_modes(summed, polys, zero_cells), polys, zero_cells)
        returned = jnp.einsum("av,axy->vxy", table, coeffs, precision=lax.Precision.HIGHEST)
        adjoint = (1.0 - relaxation_rate) * advected + relaxation_rate * returned
    return adjoint


def solution(mesh):
    in_specs = (
        P("vel", "space", None),
        P(None, "vel"),
        P(None, "vel"),
        P(None, None, "space", None),
    )
    out_specs = P("vel", "space", None)
    return jax.shard_map(shards, mesh=mesh, in_specs=in_specs, out_specs=out_specs, check_vma=False)
```

profile of v0, /device:TPU:0, one launch (start us, length us, event | category | flops | bytes accessed | tf_op | source)
XLA Modules:
  0.0 712.7 jit_solution(4509849928719995497)
XLA Ops:
  8.0 16.5 %copy.21 = f32[1024,32,128]{0,2,1:T(8,128)} copy(f32[1024,32,128]{2,1,0:T(8,128)} %param.4) | data formatting | bytes 33554432 | tf_op args[0]
  24.6 1.8 fusion.371
  26.9 34.9 %fusion.46 = f32[1024,32,128]{0,2,1:T(8,128)} fusion(f32[1024,32,128]{0,2,1:T(8,128)} %copy.21, f32[1024,32,2]{0,2,1:T(2,128)S(1)} %get-tuple-element.47, f32[1024,32,2]{0,2,1:T(2,128)S(1)} %get-tuple-element.46, f32[1024]{0:T(1024)S(1)} %bitcast.1794, pred[1024]{0:T(1024)(128)(4,1)S(1)} %get-tuple-element.6), kind=kLoop, calls=%fused_computation.70 | loop fusion | flops 50331648 | bytes 34083840 | tf_op jit(solution)/shard_map/sub | solution.py:151
  61.8 2.8 fusion.370
  64.6 3.9 collective-permute-start
  71.3 21.0 %collective-permute-done = f32[1024,2,128]{0,2,1:T(8,128)S(1)} collective-permute-done((f32[1024,2,128]{0,2,1:T(8,128)}, f32[1024,2,128]{0,2,1:T(8,128)S(1)}, u32[]{:S(2)}, u32[]{:S(2)}) %collective-permute-start) | collective-permute-done | bytes 1048608 | tf_op jit(solution)/shard_map/ppermute | solution.py:43
  92.3 22.2 %collective-permute-done.1 = f32[1024,2,128]{0,2,1:T(8,128)S(1)} collective-permute-done((f32[1024,2,128]{0,2,1:T(8,128)S(1)}, f32[1024,2,128]{0,2,1:T(8,128)S(1)}, u32[]{:S(2)}, u32[]{:S(2)}) %collective-permute-start.1) | collective-permute-done | bytes 1048608 | tf_op jit(solution)/shard_map/ppermute | solution.py:42
  114.6 27.7 %fusion.38 = f32[1024,32,128]{0,2,1:T(8,128)S(1)} fusion(f32[1024,32,128]{0,2,1:T(8,128)} %fusion.46, f32[1024,2,128]{0,2,1:T(8,128)S(1)} %collective-permute-done.1, f32[1024,2,128]{0,2,1:T(8,128)S(1)} %collective-permute-done, f32[1024]{0:T(1024)S(1)} %bitcast.1791, pred[1024]{0:T(1024)(128)(4,1)S(1)} %get-tuple-element.5), kind=kLoop, calls=%fused_computation.62 | loop fusion | flops 50331648 | bytes 35656704 | tf_op jit(solution)/shard_map/sub | solution.py:151
  142.3 23.4 %fusion.86 = f32[20,32,128]{2,0,1:T(8,128)S(1)} fusion(f32[1024,32,128]{0,2,1:T(8,128)S(1)} %fusion.38, f32[32,128]{1,0:T(8,128)S(1)} %get-tuple-element.55, f32[1024]{0:T(1024)S(1)} %bitcast.1803, f32[32,128]{1,0:T(8,128)S(1)} %get-tuple-element.56, f32[1024]{0:T(1024)S(1)} %bitcast.1800, f32[32,128]{1,0:T(8,128)S(1)} %get-tuple-element.58, ...), kind=kOutput, calls=%fused_computation.125 | convolution fusion | flops 1065353216 | bytes 17281024 | tf_op jit(solution)/shard_map/av,vxy->axy/dot_general | solution.py:195
  167.0 55.6 %all-reduce.4.cloned.1.call-done = f32[20,32,128]{2,1,0:T(8,128)} async-done(((f32[20,32,128]{2,1,0:T(8,128)}), f32[20,32,128]{2,1,0:T(8,128)}) %all-reduce.4.cloned.1.call-update) | async-done | bytes 327696 | tf_op jit(solution)/shard_map/psum | solution.py:199
  229.0 17.5 %multiply_add_fusion.2 = f32[1024,32,128]{0,2,1:T(8,128)S(1)} fusion(f32[1024,32,128]{0,2,1:T(8,128)} %copy-done.2, f32[32,128]{1,0:T(8,128)S(1)} %get-tuple-element.64, f32[32,128]{1,0:T(8,128)S(1)} %get-tuple-element.63, f32[20,32,128]{2,1,0:T(8,128)S(1)} %constant_dynamic-update-slice_fusion, f32[20,1024]{1,0:T(8,128)S(1)} %stack.12), kind=kOutput, calls=%fused_computation.124 | convolution fusion | flops 1019215872 | bytes 33996800 | tf_op jit(solution)/shard_map/av,axy->vxy/dot_general | solution.py:202
  246.5 6.2 copy-done.1
  252.9 34.8 %fusion.30 = f32[1024,32,128]{0,2,1:T(8,128)} fusion(f32[1024,32,128]{0,2,1:T(8,128)} %copy-done.1, f32[1024,32,2]{0,2,1:T(2,128)S(1)} %get-tuple-element.43, f32[1024,32,2]{0,2,1:T(2,128)S(1)} %get-tuple-element.42, f32[1024]{0:T(1024)S(1)} %bitcast.1795, pred[1024]{0:T(1024)(128)(4,1)S(1)} %get-tuple-element.6), kind=kLoop, calls=%fused_computation.54 | loop fusion | flops 50331648 | bytes 34083840 | tf_op jit(solution)/shard_map/sub | solution.py:151
  287.7 1.7 fusion.368
  289.4 2.4 collective-permute-start.2
  292.0 23.4 %collective-permute-done.2 = f32[1024,2,128]{0,2,1:T(8,128)S(1)} collective-permute-done((f32[1024,2,128]{0,2,1:T(8,128)S(1)}, f32[1024,2,128]{0,2,1:T(8,128)S(1)}, u32[]{:S(2)}, u32[]{:S(2)}) %collective-permute-start.2) | collective-permute-done | bytes 1048608 | tf_op jit(solution)/shard_map/ppermute | solution.py:43
  315.4 20.5 %collective-permute-done.3 = f32[1024,2,128]{0,2,1:T(8,128)S(1)} collective-permute-done((f32[1024,2,128]{0,2,1:T(8,128)S(1)}, f32[1024,2,128]{0,2,1:T(8,128)S(1)}, u32[]{:S(2)}, u32[]{:S(2)}) %collective-permute-start.3) | collective-permute-done | bytes 1048608 | tf_op jit(solution)/shard_map/ppermute | solution.py:42
  335.9 27.7 %fusion.22 = f32[1024,32,128]{0,2,1:T(8,128)S(1)} fusion(f32[1024,32,128]{0,2,1:T(8,128)} %fusion.30, f32[1024,2,128]{0,2,1:T(8,128)S(1)} %collective-permute-done.3, f32[1024,2,128]{0,2,1:T(8,128)S(1)} %collective-permute-done.2, f32[1024]{0:T(1024)S(1)} %bitcast.1792, pred[1024]{0:T(1024)(128)(4,1)S(1)} %get-tuple-element.5), kind=kLoop, calls=%fused_computation.46 | loop fusion | flops 50331648 | bytes 35656704 | tf_op jit(solution)/shard_map/sub | solution.py:151
  363.7 23.4 %fusion.70 = f32[20,32,128]{2,0,1:T(8,128)S(1)} fusion(f32[1024,32,128]{0,2,1:T(8,128)S(1)} %fusion.22, f32[32,128]{1,0:T(8,128)S(1)} %copy-done.9, f32[32,128]{1,0:T(8,128)S(1)} %copy-done.10, f32[32,128]{1,0:T(8,128)S(1)} %copy-done.12, f32[32,128]{1,0:T(8,128)S(1)} %copy-done.11, f32[32,128]{1,0:T(8,128)S(1)} %copy-done.8, f32[1024]{0:T(1024)S(1)} %bitcast.1804, ...), kind=kOutput, calls=%fused_computation.108 | convolution fusion | flops 1065353216 | bytes 17281024 | tf_op jit(solution)/shard_map/av,vxy->axy/dot_general | solution.py:195
  388.1 54.6 %all-reduce.6.cloned.1.call-done = f32[20,32,128]{2,1,0:T(8,128)} async-done(((f32[20,32,128]{2,1,0:T(8,128)}), f32[20,32,128]{2,1,0:T(8,128)}) %all-reduce.6.cloned.1.call-update) | async-done | bytes 327696 | tf_op jit(solution)/shard_map/psum | solution.py:199
  449.1 17.5 %multiply_add_fusion.1 = f32[1024,32,128]{0,2,1:T(8,128)S(1)} fusion(f32[1024,32,128]{0,2,1:T(8,128)} %copy-done.4, f32[32,128]{1,0:T(8,128)S(1)} %get-tuple-element.66, f32[32,128]{1,0:T(8,128)S(1)} %get-tuple-element.65, f32[20,32,128]{2,1,0:T(8,128)S(1)} %constant_dynamic-update-slice_fusion.20, f32[20,1024]{1,0:T(8,128)S(1)} %stack.12), kind=kOutput, calls=%fused_computation.107 | convolution fusion | flops 1019215872 | bytes 33996800 | tf_op jit(solution)/shard_map/av,axy->vxy/dot_general | solution.py:202
  466.6 6.2 copy-done
  473.0 34.8 %fusion.14 = f32[1024,32,128]{0,2,1:T(8,128)} fusion(f32[1024,32,128]{0,2,1:T(8,128)} %copy-done, f32[1024,32,2]{0,2,1:T(2,128)S(1)} %get-tuple-element.39, f32[1024,32,2]{0,2,1:T(2,128)S(1)} %get-tuple-element.38, f32[1024]{0:T(1024)S(1)} %bitcast.1796, pred[1024]{0:T(1024)(128)(4,1)S(1)} %get-tuple-element.6), kind=kLoop, calls=%fused_computation.38 | loop fusion | flops 50331648 | bytes 34083840 | tf_op jit(solution)/shard_map/sub | solution.py:151
  507.8 1.7 fusion.366
  509.5 2.4 collective-permute-start.4
  512.2 23.4 %collective-permute-done.4 = f32[1024,2,128]{0,2,1:T(8,128)S(1)} collective-permute-done((f32[1024,2,128]{0,2,1:T(8,128)S(1)}, f32[1024,2,128]{0,2,1:T(8,128)S(1)}, u32[]{:S(2)}, u32[]{:S(2)}) %collective-permute-start.4) | collective-permute-done | bytes 1048608 | tf_op jit(solution)/shard_map/ppermute | solution.py:43
  535.6 20.5 %collective-permute-done.5 = f32[1024,2,128]{0,2,1:T(8,128)S(1)} collective-permute-done((f32[1024,2,128]{0,2,1:T(8,128)S(1)}, f32[1024,2,128]{0,2,1:T(8,128)S(1)}, u32[]{:S(2)}, u32[]{:S(2)}) %collective-permute-start.5) | collective-permute-done | bytes 1048608 | tf_op jit(solution)/shard_map/ppermute | solution.py:42
  556.1 27.7 %fusion.6 = f32[1024,32,128]{0,2,1:T(8,128)S(1)} fusion(f32[1024,32,128]{0,2,1:T(8,128)} %fusion.14, f32[1024,2,128]{0,2,1:T(8,128)S(1)} %collective-permute-done.5, f32[1024,2,128]{0,2,1:T(8,128)S(1)} %collective-permute-done.4, f32[1024]{0:T(1024)S(1)} %bitcast.1793, pred[1024]{0:T(1024)(128)(4,1)S(1)} %get-tuple-element.5), kind=kLoop, calls=%fused_computation.30 | loop fusion | flops 50331648 | bytes 35656704 | tf_op jit(solution)/shard_map/sub | solution.py:151
  583.8 23.4 %fusion.54 = f32[20,32,128]{2,0,1:T(8,128)S(1)} fusion(f32[1024,32,128]{0,2,1:T(8,128)S(1)} %fusion.6, f32[32,128]{1,0:T(8,128)S(1)} %copy-done.6, f32[32,128]{1,0:T(8,128)S(1)} %copy-done.7, f32[32,128]{1,0:T(8,128)S(1)} %get-tuple-element.60, f32[32,128]{1,0:T(8,128)S(1)} %get-tuple-element.51, f32[32,128]{1,0:T(8,128)S(1)} %get-tuple-element.48, ...), kind=kOutput, calls=%fused_computation.91 | convolution fusion | flops 1065353216 | bytes 17281024 | tf_op jit(solution)/shard_map/av,vxy->axy/dot_general | solution.py:195
  608.0 54.9 %all-reduce.8.cloned.1.call-done = f32[20,32,128]{2,1,0:T(8,128)} async-done(((f32[20,32,128]{2,1,0:T(8,128)}), f32[20,32,128]{2,1,0:T(8,128)}) %all-reduce.8.cloned.1.call-update) | async-done | bytes 327696 | tf_op jit(solution)/shard_map/psum | solution.py:199
  669.2 19.1 %multiply_add_fusion = f32[1024,32,128]{0,2,1:T(8,128)} fusion(f32[1024,32,128]{0,2,1:T(8,128)} %copy-done.3, f32[32,128]{1,0:T(8,128)S(1)} %get-tuple-element.15, f32[32,128]{1,0:T(8,128)S(1)} %get-tuple-element.14, f32[20,32,128]{2,1,0:T(8,128)S(1)} %constant_dynamic-update-slice_fusion.40, f32[20,1024]{1,0:T(8,128)S(1)} %stack.12), kind=kOutput, calls=%fused_computation.90 | convolution fusion | flops 1019215872 | bytes 33996800 | tf_op jit(solution)/shard_map/av,axy->vxy/dot_general | solution.py:202
  688.3 17.4 %copy.32 = f32[1024,32,128]{2,1,0:T(8,128)} copy(f32[1024,32,128]{0,2,1:T(8,128)} %multiply_add_fusion) | data formatting | bytes 33554432 | tf_op jit(solution)/shard_map/add | solution.py:203
  (113 shorter events, 27.8 us)
Async XLA Ops:
  6.5 216.1 %all-reduce.4.cloned.1.call-start = ((), (), s32[]{:S(2)}) async-start(), calls=%async_computation | async-start | bytes 655360 | tf_op jit(solution)/shard_map/psum | solution.py:199
  26.9 43.7 %copy-start.5 = (f32[3,5,32,128]{3,2,1,0:T(8,128)S(1)}, f32[3,5,32,128]{3,2,1,0:T(8,128)}, u32[]{:S(2)}) copy-start(f32[3,5,32,128]{3,2,1,0:T(8,128)} %param.7) | copy-start | bytes 737284
  64.6 27.8 %collective-permute-start = (f32[1024,2,128]{0,2,1:T(8,128)}, f32[1024,2,128]{0,2,1:T(8,128)S(1)}, u32[]{:S(2)}, u32[]{:S(2)}) collective-permute-start(f32[1024,2,128]{0,2,1:T(8,128)} %get-tuple-element.44), channel_id=1, source_target_pairs={{8,0},{16,8},{24,16},{0,24},{9,1},{17,9},{25,17},{1,25},{10,2},{18... | collective-permute-start | bytes 3145736 | tf_op jit(solution)/shard_map/ppermute | solution.py:43
  68.5 46.1 %collective-permute-start.1 = (f32[1024,2,128]{0,2,1:T(8,128)S(1)}, f32[1024,2,128]{0,2,1:T(8,128)S(1)}, u32[]{:S(2)}, u32[]{:S(2)}) collective-permute-start(f32[1024,2,128]{0,2,1:T(8,128)S(1)} %get-tuple-element.45), channel_id=1, source_target_pairs={{0,8},{8,16},{16,24},{24,0},{1,9},{9,17},{17,25},{25,1},{2,10},{10... | collective-permute-start | bytes 3145736 | tf_op jit(solution)/shard_map/ppermute | solution.py:42
  114.6 27.7 %copy-start.13 = (f32[1,1024]{1,0:T(1,128)S(1)}, f32[1,1024]{1,0:T(1,128)}, u32[]{:S(2)}) copy-start(f32[1,1024]{1,0:T(1,128)} %get-tuple-element.88) | copy-start | bytes 12292
  114.6 27.7 %copy-start.14 = (f32[1,1024]{1,0:T(1,128)S(1)}, f32[1,1024]{1,0:T(1,128)}, u32[]{:S(2)}) copy-start(f32[1,1024]{1,0:T(1,128)} %get-tuple-element.89) | copy-start | bytes 12292
  114.6 27.7 %copy-start.15 = (f32[1,1024]{1,0:T(1,128)S(1)}, f32[1,1024]{1,0:T(1,128)}, u32[]{:S(2)}) copy-start(f32[1,1024]{1,0:T(1,128)} %get-tuple-element.90) | copy-start | bytes 12292
  142.2 23.4 %copy-start.2 = (f32[1024,32,128]{0,2,1:T(8,128)}, f32[1024,32,128]{0,2,1:T(8,128)S(1)}, u32[]{:S(2)}) copy-start(f32[1024,32,128]{0,2,1:T(8,128)S(1)} %fusion.38) | copy-start | bytes 50331652
  166.5 276.3 %all-reduce.6.cloned.1.call-start = ((), (), s32[]{:S(2)}) async-start(), calls=%async_computation.1 | async-start | bytes 655360 | tf_op jit(solution)/shard_map/psum | solution.py:199
  246.5 6.2 copy-start.1
  289.4 26.1 %collective-permute-start.2 = (f32[1024,2,128]{0,2,1:T(8,128)S(1)}, f32[1024,2,128]{0,2,1:T(8,128)S(1)}, u32[]{:S(2)}, u32[]{:S(2)}) collective-permute-start(f32[1024,2,128]{0,2,1:T(8,128)S(1)} %get-tuple-element.40), channel_id=1, source_target_pairs={{8,0},{16,8},{24,16},{0,24},{9,1},{17,9},{25,17},{1,25},{10,2},{18... | collective-permute-start | bytes 3145736 | tf_op jit(solution)/shard_map/ppermute | solution.py:43
  291.8 71.8 %copy-start.8 = (f32[32,128]{1,0:T(8,128)S(1)}, f32[32,128]{1,0:T(8,128)}, u32[]{:S(2)}) copy-start(f32[32,128]{1,0:T(8,128)} %get-tuple-element.49) | copy-start | bytes 49156
  291.8 71.9 %copy-start.9 = (f32[32,128]{1,0:T(8,128)S(1)}, f32[32,128]{1,0:T(8,128)}, u32[]{:S(2)}) copy-start(f32[32,128]{1,0:T(8,128)} %get-tuple-element.52) | copy-start | bytes 49156
  291.8 71.9 %copy-start.10 = (f32[32,128]{1,0:T(8,128)S(1)}, f32[32,128]{1,0:T(8,128)}, u32[]{:S(2)}) copy-start(f32[32,128]{1,0:T(8,128)} %get-tuple-element.53) | copy-start | bytes 49156
  291.8 71.9 %copy-start.11 = (f32[32,128]{1,0:T(8,128)S(1)}, f32[32,128]{1,0:T(8,128)}, u32[]{:S(2)}) copy-start(f32[32,128]{1,0:T(8,128)} %get-tuple-element.54) | copy-start | bytes 49156
  291.8 71.9 %copy-start.12 = (f32[32,128]{1,0:T(8,128)S(1)}, f32[32,128]{1,0:T(8,128)}, u32[]{:S(2)}) copy-start(f32[32,128]{1,0:T(8,128)} %get-tuple-element.59) | copy-start | bytes 49156
  291.8 44.1 %collective-permute-start.3 = (f32[1024,2,128]{0,2,1:T(8,128)S(1)}, f32[1024,2,128]{0,2,1:T(8,128)S(1)}, u32[]{:S(2)}, u32[]{:S(2)}) collective-permute-start(f32[1024,2,128]{0,2,1:T(8,128)S(1)} %get-tuple-element.41), channel_id=1, source_target_pairs={{0,8},{8,16},{16,24},{24,0},{1,9},{9,17},{17,25},{25,1},{2,10},{10... | collective-permute-start | bytes 3145736 | tf_op jit(solution)/shard_map/ppermute | solution.py:42
  363.6 23.5 %copy-start.4 = (f32[1024,32,128]{0,2,1:T(8,128)}, f32[1024,32,128]{0,2,1:T(8,128)S(1)}, u32[]{:S(2)}) copy-start(f32[1024,32,128]{0,2,1:T(8,128)S(1)} %fusion.22) | copy-start | bytes 50331652
  387.9 275.0 %all-reduce.8.cloned.1.call-start = ((), (), s32[]{:S(2)}) async-start(), calls=%async_computation.2 | async-start | bytes 655360 | tf_op jit(solution)/shard_map/psum | solution.py:199
  466.6 6.2 copy-start
  509.5 26.1 %collective-permute-start.4 = (f32[1024,2,128]{0,2,1:T(8,128)S(1)}, f32[1024,2,128]{0,2,1:T(8,128)S(1)}, u32[]{:S(2)}, u32[]{:S(2)}) collective-permute-start(f32[1024,2,128]{0,2,1:T(8,128)S(1)} %get-tuple-element.36), channel_id=1, source_target_pairs={{8,0},{16,8},{24,16},{0,24},{9,1},{17,9},{25,17},{1,25},{10,2},{18... | collective-permute-start | bytes 3145736 | tf_op jit(solution)/shard_map/ppermute | solution.py:43
  511.9 71.8 %copy-start.6 = (f32[32,128]{1,0:T(8,128)S(1)}, f32[32,128]{1,0:T(8,128)}, u32[]{:S(2)}) copy-start(f32[32,128]{1,0:T(8,128)} %get-tuple-element.61) | copy-start | bytes 49156
  511.9 71.9 %copy-start.7 = (f32[32,128]{1,0:T(8,128)S(1)}, f32[32,128]{1,0:T(8,128)}, u32[]{:S(2)}) copy-start(f32[32,128]{1,0:T(8,128)} %get-tuple-element.62) | copy-start | bytes 49156
  511.9 44.2 %collective-permute-start.5 = (f32[1024,2,128]{0,2,1:T(8,128)S(1)}, f32[1024,2,128]{0,2,1:T(8,128)S(1)}, u32[]{:S(2)}, u32[]{:S(2)}) collective-permute-start(f32[1024,2,128]{0,2,1:T(8,128)S(1)} %get-tuple-element.37), channel_id=1, source_target_pairs={{0,8},{8,16},{16,24},{24,0},{1,9},{9,17},{17,25},{25,1},{2,10},{10... | collective-permute-start | bytes 3145736 | tf_op jit(solution)/shard_map/ppermute | solution.py:42
  583.7 23.4 %copy-start.3 = (f32[1024,32,128]{0,2,1:T(8,128)}, f32[1024,32,128]{0,2,1:T(8,128)S(1)}, u32[]{:S(2)}) copy-start(f32[1024,32,128]{0,2,1:T(8,128)S(1)} %fusion.6) | copy-start | bytes 50331652
Sparse Core Ops, SparseCore 0:
  166.6 55.9 all-reduce.3
  388.0 54.6 all-reduce.5
  608.1 54.6 all-reduce.7
where the time goes:
time: 724 us; the launch traced here: 713 us
  waiting for transfers between devices  296 us (41%)
  other arithmetic  210 us (29%)
  matrix products  124 us (17%)
  local copies, waits for them, and re-layouts  58.5 us (8%)
  between operations  14.2 us (2%)
  starting transfers between devices  10 us (1%)
    sub x6, other arithmetic, upwind_back(): return center - 0.5 * lam_col * (3.0 * center - 4.0 * nearer + farther)  187 us
    psum x3, waiting for transfers between devices, shards(): summed = lax.psum(raw_moments, 'vel')  165 us
    dot_general x3, matrix products, shards(): jnp.einsum('av,vxy->axy', table, weight * advected, precision=lax.Precisi...  70.1 us
    ppermute x3, waiting for transfers between devices, with_halo(): after = lax.ppermute(first, axis, down)  67.8 us
    ppermute x3, waiting for transfers between devices, with_halo(): before = lax.ppermute(last, axis, up)  63.2 us
    dot_general x3, matrix products, shards(): jnp.einsum('av,axy->vxy', table, coeffs, precision=lax.Precision.HIGHEST)  54.2 us
    unnamed x36, local copies, waits for them, and re-layouts  28.9 us
    unnamed x54, other arithmetic  18.7 us
  transfers between devices with their start and end apart: 9, of which 9 were waited for; matrix products, arithmetic and copies ran while one was open for 0% of the time, Pallas kernels for 0%

commit v1 on v0

--- a/solution.py
+++ b/solution.py
@@ -196,7 +196,8 @@
             "av,vxy->axy", table, weight * advected, precision=lax.Precision.HIGHEST
         )
         zero_cells = jnp.zeros_like(particle_concentration)
-        summed = lax.psum(raw_moments, "vel")
+        parts = lax.all_gather(raw_moments, "vel", axis=0, tiled=False)
+        summed = parts.sum(axis=0)
         polys = hermite_polys(flow_rows, reciprocal_factor)
         coeffs = to_coeffs(to_modes(summed, polys, zero_cells), polys, zero_cells)
         returned = jnp.einsum("av,axy->vxy", table, coeffs, precision=lax.Precision.HIGHEST)

time: 724 us -> 647 us (0.89)
  waiting for transfers between devices: 296 us -> 236 us
  other arithmetic: 210 us -> 197 us
    psum x3 -> x0, waiting for transfers between devices: 165 us -> none  [shards(): summed = lax.psum(raw_moments, 'vel')]
    all_gather x0 -> x3, waiting for transfers between devices: none -> 97.5 us  [shards(): parts = lax.all_gather(raw_moments, 'vel', axis=0, tiled=False)]
    unnamed x54, other arithmetic: 18.7 us -> 1.74 us
    unnamed x36 -> x16, local copies, waits for them, and re-layouts: 28.9 us -> 28.9 us
where the time goes in v1:
time: 647 us; the launch traced here: 638 us
  waiting for transfers between devices  236 us (36%)
  other arithmetic  197 us (30%)
  matrix products  124 us (19%)
  local copies, waits for them, and re-layouts  57.5 us (9%)
  between operations  14.2 us (2%)
  starting transfers between devices  9.94 us (2%)
    sub x6, other arithmetic, upwind_back(): return center - 0.5 * lam_col * (3.0 * center - 4.0 * nearer + farther)  187 us
    all_gather x3, waiting for transfers between devices, shards(): parts = lax.all_gather(raw_moments, 'vel', axis=0, tiled=False)  97.5 us
    ppermute x3, waiting for transfers between devices, with_halo(): after = lax.ppermute(first, axis, down)  70.5 us
    dot_general x3, matrix products, shards(): jnp.einsum('av,vxy->axy', table, weight * advected, precision=lax.Precisi...  70.1 us
    ppermute x3, waiting for transfers between devices, with_halo(): before = lax.ppermute(last, axis, up)  67.5 us
    dot_general x3, matrix products, shards(): jnp.einsum('av,axy->vxy', table, coeffs, precision=lax.Precision.HIGHEST)  54.2 us
    unnamed x16, local copies, waits for them, and re-layouts  28.9 us
    add x1, local copies, waits for them, and re-layouts, shards(): adjoint = (1.0 - relaxation_rate) * advected + relaxation_rate * returned  17.4 us
  transfers between devices with their start and end apart: 9, of which 9 were waited for; matrix products, arithmetic and copies ran while one was open for 0% of the time, Pallas kernels for 0%

profile of v1, /device:TPU:0, one launch (start us, length us, event | category | flops | bytes accessed | tf_op | source)
XLA Modules:
  0.0 638.0 jit_solution(11818337508419835612)
XLA Ops:
  8.0 16.5 %copy.106 = f32[1024,32,128]{0,2,1:T(8,128)} copy(f32[1024,32,128]{2,1,0:T(8,128)} %param.4) | data formatting | bytes 33554432 | tf_op args[0]
  26.4 34.8 %fusion.46 = f32[1024,32,128]{0,2,1:T(8,128)} fusion(f32[1024,32,128]{0,2,1:T(8,128)} %copy.106, f32[1024,32,2]{0,2,1:T(2,128)S(1)} %get-tuple-element.47, f32[1024,32,2]{0,2,1:T(2,128)S(1)} %get-tuple-element.46, f32[1024]{0:T(1024)S(1)} %bitcast.1800, pred[1024]{0:T(1024)(128)(4,1)S(1)} %get-tuple-element.6), kind=kLoop, calls=%fused_computation.70 | loop fusion | flops 50331648 | bytes 34083840 | tf_op jit(solution)/shard_map/sub | solution.py:151
  61.2 3.1 fusion.370
  64.3 3.9 collective-permute-start
  68.5 23.6 %collective-permute-done = f32[1024,2,128]{0,2,1:T(8,128)S(1)} collective-permute-done((f32[1024,2,128]{0,2,1:T(8,128)}, f32[1024,2,128]{0,2,1:T(8,128)S(1)}, u32[]{:S(2)}, u32[]{:S(2)}) %collective-permute-start) | collective-permute-done | bytes 1048608 | tf_op jit(solution)/shard_map/ppermute | solution.py:43
  92.1 22.2 %collective-permute-done.1 = f32[1024,2,128]{0,2,1:T(8,128)S(1)} collective-permute-done((f32[1024,2,128]{0,2,1:T(8,128)}, f32[1024,2,128]{0,2,1:T(8,128)S(1)}, u32[]{:S(2)}, u32[]{:S(2)}) %collective-permute-start.1) | collective-permute-done | bytes 1048608 | tf_op jit(solution)/shard_map/ppermute | solution.py:42
  114.3 27.5 %fusion.38 = f32[1024,32,128]{0,2,1:T(8,128)S(1)} fusion(f32[1024,32,128]{0,2,1:T(8,128)} %fusion.46, f32[1024,2,128]{0,2,1:T(8,128)S(1)} %collective-permute-done.1, f32[1024,2,128]{0,2,1:T(8,128)S(1)} %collective-permute-done, f32[1024]{0:T(1024)S(1)} %bitcast.1797, pred[1024]{0:T(1024)(128)(4,1)S(1)} %get-tuple-element.5), kind=kLoop, calls=%fused_computation.62 | loop fusion | flops 50331648 | bytes 35656704 | tf_op jit(solution)/shard_map/sub | solution.py:151
  141.9 23.4 %fusion.86 = f32[20,32,128]{2,0,1:T(8,128)S(1)} fusion(f32[1024,32,128]{0,2,1:T(8,128)S(1)} %fusion.38, f32[32,128]{1,0:T(8,128)S(1)} %get-tuple-element.55, f32[1024]{0:T(1024)S(1)} %bitcast.1809, f32[32,128]{1,0:T(8,128)S(1)} %get-tuple-element.56, f32[1024]{0:T(1024)S(1)} %bitcast.1806, f32[32,128]{1,0:T(8,128)S(1)} %get-tuple-element.58, ...), kind=kOutput, calls=%fused_computation.125 | convolution fusion | flops 1065353216 | bytes 17281024 | tf_op jit(solution)/shard_map/av,vxy->axy/dot_general | solution.py:195
  166.7 33.6 %all-gather.7.cloned.1.call-done = f32[160,32,128]{2,1,0:T(8,128)} async-done(((f32[20,32,128]{2,1,0:T(8,128)}), f32[160,32,128]{2,1,0:T(8,128)}) %all-gather.7.cloned.1.call-update) | async-done | bytes 2621456 | tf_op jit(solution)/shard_map/all_gather | solution.py:199
  200.3 2.0 reduce_sum.27
  203.0 17.5 %multiply_add_fusion.2 = f32[1024,32,128]{0,2,1:T(8,128)S(1)} fusion(f32[1024,32,128]{0,2,1:T(8,128)} %copy-done.3, f32[32,128]{1,0:T(8,128)S(1)} %get-tuple-element.64, f32[32,128]{1,0:T(8,128)S(1)} %get-tuple-element.63, f32[20,32,128]{2,1,0:T(8,128)S(1)} %constant_dynamic-update-slice_fusion, f32[20,1024]{1,0:T(8,128)S(1)} %stack.12), kind=kOutput, calls=%fused_computation.124 | convolution fusion | flops 1019215872 | bytes 33996800 | tf_op jit(solution)/shard_map/av,axy->vxy/dot_general | solution.py:203
  220.6 6.2 copy-done.1
  227.0 34.8 %fusion.30 = f32[1024,32,128]{0,2,1:T(8,128)} fusion(f32[1024,32,128]{0,2,1:T(8,128)} %copy-done.1, f32[1024,32,2]{0,2,1:T(2,128)S(1)} %get-tuple-element.43, f32[1024,32,2]{0,2,1:T(2,128)S(1)} %get-tuple-element.42, f32[1024]{0:T(1024)S(1)} %bitcast.1801, pred[1024]{0:T(1024)(128)(4,1)S(1)} %get-tuple-element.6), kind=kLoop, calls=%fused_computation.54 | loop fusion | flops 50331648 | bytes 34083840 | tf_op jit(solution)/shard_map/sub | solution.py:151
  263.4 2.4 collective-permute-start.2
  266.0 23.5 %collective-permute-done.2 = f32[1024,2,128]{0,2,1:T(8,128)S(1)} collective-permute-done((f32[1024,2,128]{0,2,1:T(8,128)S(1)}, f32[1024,2,128]{0,2,1:T(8,128)S(1)}, u32[]{:S(2)}, u32[]{:S(2)}) %collective-permute-start.2) | collective-permute-done | bytes 1048608 | tf_op jit(solution)/shard_map/ppermute | solution.py:43
  289.5 22.6 %collective-permute-done.3 = f32[1024,2,128]{0,2,1:T(8,128)S(1)} collective-permute-done((f32[1024,2,128]{0,2,1:T(8,128)S(1)}, f32[1024,2,128]{0,2,1:T(8,128)S(1)}, u32[]{:S(2)}, u32[]{:S(2)}) %collective-permute-start.3) | collective-permute-done | bytes 1048608 | tf_op jit(solution)/shard_map/ppermute | solution.py:42
  312.1 27.5 %fusion.22 = f32[1024,32,128]{0,2,1:T(8,128)S(1)} fusion(f32[1024,32,128]{0,2,1:T(8,128)} %fusion.30, f32[1024,2,128]{0,2,1:T(8,128)S(1)} %collective-permute-done.3, f32[1024,2,128]{0,2,1:T(8,128)S(1)} %collective-permute-done.2, f32[1024]{0:T(1024)S(1)} %bitcast.1798, pred[1024]{0:T(1024)(128)(4,1)S(1)} %get-tuple-element.5), kind=kLoop, calls=%fused_computation.46 | loop fusion | flops 50331648 | bytes 35656704 | tf_op jit(solution)/shard_map/sub | solution.py:151
  339.7 23.4 %fusion.70 = f32[20,32,128]{2,0,1:T(8,128)S(1)} fusion(f32[1024,32,128]{0,2,1:T(8,128)S(1)} %fusion.22, f32[32,128]{1,0:T(8,128)S(1)} %get-tuple-element.52, f32[32,128]{1,0:T(8,128)S(1)} %get-tuple-element.53, f32[32,128]{1,0:T(8,128)S(1)} %get-tuple-element.59, f32[32,128]{1,0:T(8,128)S(1)} %get-tuple-element.54, f32[32,128]{1,0:T(8,128)S(1)} %get-tuple-element.49, ...), kind=kOutput, calls=%fused_computation.108 | convolution fusion | flops 1065353216 | bytes 17281024 | tf_op jit(solution)/shard_map/av,vxy->axy/dot_general | solution.py:195
  364.2 31.8 %all-gather.9.cloned.1.call-done = f32[160,32,128]{2,1,0:T(8,128)} async-done(((f32[20,32,128]{2,1,0:T(8,128)}), f32[160,32,128]{2,1,0:T(8,128)}) %all-gather.9.cloned.1.call-update) | async-done | bytes 2621456 | tf_op jit(solution)/shard_map/all_gather | solution.py:199
  396.0 2.0 reduce_sum.28
  398.8 17.5 %multiply_add_fusion.1 = f32[1024,32,128]{0,2,1:T(8,128)S(1)} fusion(f32[1024,32,128]{0,2,1:T(8,128)} %copy-done.4, f32[32,128]{1,0:T(8,128)S(1)} %get-tuple-element.66, f32[32,128]{1,0:T(8,128)S(1)} %get-tuple-element.65, f32[20,32,128]{2,1,0:T(8,128)S(1)} %constant_dynamic-update-slice_fusion.20, f32[20,1024]{1,0:T(8,128)S(1)} %stack.12), kind=kOutput, calls=%fused_computation.107 | convolution fusion | flops 1019215872 | bytes 33996800 | tf_op jit(solution)/shard_map/av,axy->vxy/dot_general | solution.py:203
  416.3 6.2 copy-done
  422.7 34.8 %fusion.14 = f32[1024,32,128]{0,2,1:T(8,128)} fusion(f32[1024,32,128]{0,2,1:T(8,128)} %copy-done, f32[1024,32,2]{0,2,1:T(2,128)S(1)} %get-tuple-element.39, f32[1024,32,2]{0,2,1:T(2,128)S(1)} %get-tuple-element.38, f32[1024]{0:T(1024)S(1)} %bitcast.1802, pred[1024]{0:T(1024)(128)(4,1)S(1)} %get-tuple-element.6), kind=kLoop, calls=%fused_computation.38 | loop fusion | flops 50331648 | bytes 34083840 | tf_op jit(solution)/shard_map/sub | solution.py:151
  459.2 2.4 collective-permute-start.4
  461.8 23.4 %collective-permute-done.4 = f32[1024,2,128]{0,2,1:T(8,128)S(1)} collective-permute-done((f32[1024,2,128]{0,2,1:T(8,128)S(1)}, f32[1024,2,128]{0,2,1:T(8,128)S(1)}, u32[]{:S(2)}, u32[]{:S(2)}) %collective-permute-start.4) | collective-permute-done | bytes 1048608 | tf_op jit(solution)/shard_map/ppermute | solution.py:43
  485.2 22.6 %collective-permute-done.5 = f32[1024,2,128]{0,2,1:T(8,128)S(1)} collective-permute-done((f32[1024,2,128]{0,2,1:T(8,128)S(1)}, f32[1024,2,128]{0,2,1:T(8,128)S(1)}, u32[]{:S(2)}, u32[]{:S(2)}) %collective-permute-start.5) | collective-permute-done | bytes 1048608 | tf_op jit(solution)/shard_map/ppermute | solution.py:42
  507.9 27.5 %fusion.6 = f32[1024,32,128]{0,2,1:T(8,128)S(1)} fusion(f32[1024,32,128]{0,2,1:T(8,128)} %fusion.14, f32[1024,2,128]{0,2,1:T(8,128)S(1)} %collective-permute-done.5, f32[1024,2,128]{0,2,1:T(8,128)S(1)} %collective-permute-done.4, f32[1024]{0:T(1024)S(1)} %bitcast.1799, pred[1024]{0:T(1024)(128)(4,1)S(1)} %get-tuple-element.5), kind=kLoop, calls=%fused_computation.30 | loop fusion | flops 50331648 | bytes 35656704 | tf_op jit(solution)/shard_map/sub | solution.py:151
  535.4 23.4 %fusion.54 = f32[20,32,128]{2,0,1:T(8,128)S(1)} fusion(f32[1024,32,128]{0,2,1:T(8,128)S(1)} %fusion.6, f32[32,128]{1,0:T(8,128)S(1)} %get-tuple-element.61, f32[32,128]{1,0:T(8,128)S(1)} %get-tuple-element.62, f32[32,128]{1,0:T(8,128)S(1)} %get-tuple-element.60, f32[32,128]{1,0:T(8,128)S(1)} %get-tuple-element.51, f32[32,128]{1,0:T(8,128)S(1)} %get-tuple-element.48, ...), kind=kOutput, calls=%fused_computation.91 | convolution fusion | flops 1065353216 | bytes 17281024 | tf_op jit(solution)/shard_map/av,vxy->axy/dot_general | solution.py:195
  559.7 32.1 %all-gather.11.cloned.1.call-done = f32[160,32,128]{2,1,0:T(8,128)} async-done(((f32[20,32,128]{2,1,0:T(8,128)}), f32[160,32,128]{2,1,0:T(8,128)}) %all-gather.11.cloned.1.call-update) | async-done | bytes 2621456 | tf_op jit(solution)/shard_map/all_gather | solution.py:199
  591.8 2.0 reduce_sum.29
  594.5 19.1 %multiply_add_fusion = f32[1024,32,128]{0,2,1:T(8,128)} fusion(f32[1024,32,128]{0,2,1:T(8,128)} %copy-done.2, f32[32,128]{1,0:T(8,128)S(1)} %get-tuple-element.15, f32[32,128]{1,0:T(8,128)S(1)} %get-tuple-element.14, f32[20,32,128]{2,1,0:T(8,128)S(1)} %constant_dynamic-update-slice_fusion.40, f32[20,1024]{1,0:T(8,128)S(1)} %stack.12), kind=kOutput, calls=%fused_computation.90 | convolution fusion | flops 1019215872 | bytes 33996800 | tf_op jit(solution)/shard_map/av,axy->vxy/dot_general | solution.py:203
  613.7 17.4 %copy.117 = f32[1024,32,128]{2,1,0:T(8,128)} copy(f32[1024,32,128]{0,2,1:T(8,128)} %multiply_add_fusion) | data formatting | bytes 33554432 | tf_op jit(solution)/shard_map/add | solution.py:204
  (96 shorter events, 12.8 us)
Async XLA Ops:
  6.5 193.7 %all-gather.7.cloned.1.call-start = ((), (), s32[]{:S(2)}) async-start(), calls=%async_computation | async-start | bytes 2949120 | tf_op jit(solution)/shard_map/all_gather | solution.py:199
  26.4 42.1 %copy-start.5 = (f32[3,5,32,128]{3,2,1,0:T(8,128)S(1)}, f32[3,5,32,128]{3,2,1,0:T(8,128)}, u32[]{:S(2)}) copy-start(f32[3,5,32,128]{3,2,1,0:T(8,128)} %param.7) | copy-start | bytes 737284
  64.3 27.8 %collective-permute-start = (f32[1024,2,128]{0,2,1:T(8,128)}, f32[1024,2,128]{0,2,1:T(8,128)S(1)}, u32[]{:S(2)}, u32[]{:S(2)}) collective-permute-start(f32[1024,2,128]{0,2,1:T(8,128)} %get-tuple-element.44), channel_id=1, source_target_pairs={{8,0},{16,8},{24,16},{0,24},{9,1},{17,9},{25,17},{1,25},{10,2},{18... | collective-permute-start | bytes 3145736 | tf_op jit(solution)/shard_map/ppermute | solution.py:43
  68.3 46.1 %collective-permute-start.1 = (f32[1024,2,128]{0,2,1:T(8,128)}, f32[1024,2,128]{0,2,1:T(8,128)S(1)}, u32[]{:S(2)}, u32[]{:S(2)}) collective-permute-start(f32[1024,2,128]{0,2,1:T(8,128)} %get-tuple-element.45), channel_id=1, source_target_pairs={{0,8},{8,16},{16,24},{24,0},{1,9},{9,17},{17,25},{25,1},{2,10},{10... | collective-permute-start | bytes 3145736 | tf_op jit(solution)/shard_map/ppermute | solution.py:42
  141.9 23.4 %copy-start.3 = (f32[1024,32,128]{0,2,1:T(8,128)}, f32[1024,32,128]{0,2,1:T(8,128)S(1)}, u32[]{:S(2)}) copy-start(f32[1024,32,128]{0,2,1:T(8,128)S(1)} %fusion.38) | copy-start | bytes 50331652
  166.1 229.9 %all-gather.9.cloned.1.call-start = ((), (), s32[]{:S(2)}) async-start(), calls=%async_computation.1 | async-start | bytes 2949120 | tf_op jit(solution)/shard_map/all_gather | solution.py:199
  220.6 6.2 copy-start.1
  263.4 26.1 %collective-permute-start.2 = (f32[1024,2,128]{0,2,1:T(8,128)S(1)}, f32[1024,2,128]{0,2,1:T(8,128)S(1)}, u32[]{:S(2)}, u32[]{:S(2)}) collective-permute-start(f32[1024,2,128]{0,2,1:T(8,128)S(1)} %get-tuple-element.40), channel_id=1, source_target_pairs={{8,0},{16,8},{24,16},{0,24},{9,1},{17,9},{25,17},{1,25},{10,2},{18... | collective-permute-start | bytes 3145736 | tf_op jit(solution)/shard_map/ppermute | solution.py:43
  265.9 46.3 %collective-permute-start.3 = (f32[1024,2,128]{0,2,1:T(8,128)S(1)}, f32[1024,2,128]{0,2,1:T(8,128)S(1)}, u32[]{:S(2)}, u32[]{:S(2)}) collective-permute-start(f32[1024,2,128]{0,2,1:T(8,128)S(1)} %get-tuple-element.41), channel_id=1, source_target_pairs={{0,8},{8,16},{16,24},{24,0},{1,9},{9,17},{17,25},{25,1},{2,10},{10... | collective-permute-start | bytes 3145736 | tf_op jit(solution)/shard_map/ppermute | solution.py:42
  339.7 23.4 %copy-start.4 = (f32[1024,32,128]{0,2,1:T(8,128)}, f32[1024,32,128]{0,2,1:T(8,128)S(1)}, u32[]{:S(2)}) copy-start(f32[1024,32,128]{0,2,1:T(8,128)S(1)} %fusion.22) | copy-start | bytes 50331652
  363.9 227.8 %all-gather.11.cloned.1.call-start = ((), (), s32[]{:S(2)}) async-start(), calls=%async_computation.2 | async-start | bytes 2949120 | tf_op jit(solution)/shard_map/all_gather | solution.py:199
  416.3 6.2 copy-start
  459.2 26.1 %collective-permute-start.4 = (f32[1024,2,128]{0,2,1:T(8,128)S(1)}, f32[1024,2,128]{0,2,1:T(8,128)S(1)}, u32[]{:S(2)}, u32[]{:S(2)}) collective-permute-start(f32[1024,2,128]{0,2,1:T(8,128)S(1)} %get-tuple-element.36), channel_id=1, source_target_pairs={{8,0},{16,8},{24,16},{0,24},{9,1},{17,9},{25,17},{1,25},{10,2},{18... | collective-permute-start | bytes 3145736 | tf_op jit(solution)/shard_map/ppermute | solution.py:43
  461.6 46.3 %collective-permute-start.5 = (f32[1024,2,128]{0,2,1:T(8,128)S(1)}, f32[1024,2,128]{0,2,1:T(8,128)S(1)}, u32[]{:S(2)}, u32[]{:S(2)}) collective-permute-start(f32[1024,2,128]{0,2,1:T(8,128)S(1)} %get-tuple-element.37), channel_id=1, source_target_pairs={{0,8},{8,16},{16,24},{24,0},{1,9},{9,17},{17,25},{25,1},{2,10},{10... | collective-permute-start | bytes 3145736 | tf_op jit(solution)/shard_map/ppermute | solution.py:42
  535.4 23.4 %copy-start.2 = (f32[1024,32,128]{0,2,1:T(8,128)}, f32[1024,32,128]{0,2,1:T(8,128)S(1)}, u32[]{:S(2)}) copy-start(f32[1024,32,128]{0,2,1:T(8,128)S(1)} %fusion.6) | copy-start | bytes 50331652
Sparse Core Ops, SparseCore 0:
  166.3 33.9 all-gather.6
  364.1 31.9 all-gather.8
  559.8 31.9 all-gather.10
